TPU v7x, 32 devices: a whole 2x2x4 slice. The times are simulated.
32 devices in a mesh: grp: 4 (over y, core), dev: 8 (over z, x).
Axes of the slice: x: 2, y: 2, z: 4, core: 2. Of those that a mesh axis runs over, the one named last changes fastest.
Arguments:
- embeddings: bfloat16 [8192, 768], P(('grp', 'dev')), may hold values from -6 to 6
- language: int32 [8192], P(('grp', 'dev')), may hold values from 0 to 108
- sentence_group: int32 [8192], P(('grp', 'dev')), may hold values from 0 to 2047
- pair_mask: int32 [109, 109], replicated, may hold values 0 or 1
Outputs:
- gradient: float32 [8192, 768], P(('grp', 'dev'))
All inputs are finite; a program needn't handle non-finite values.
Results may differ from a plain program's by a relative error of at most 0.0012.
Values may be sent and summed in bfloat16 or wider, within the bound.
A program may use at most 256 MiB of HBM per device.

v0:
```python
import math

import jax
import jax.numpy as jnp
from jax import lax
from jax.sharding import PartitionSpec as P


def language_onehot(labels_lang, lang_count):
    return (labels_lang[..., None] == jnp.arange(lang_count, dtype=jnp.int32)).astype(jnp.float32)


def coefficients(scores, packed_a, packed_b, weight_table, scale):
    lang_count = weight_table.shape[0]
    onehot_a = language_onehot(packed_a % lang_count, lang_count)
    second_language_indicator = language_onehot(packed_b % lang_count, lang_count)
    group_a = packed_a // lang_count
    group_b = packed_b // lang_count
    weight_applied_terms = jnp.einsum(
        "prl,lm->prm", onehot_a, weight_table, precision=lax.Precision.HIGHEST
    )
    weight_values = jnp.einsum(
        "auk,ack->auc",
        weight_applied_terms,
        second_language_indicator,
        precision=lax.Precision.HIGHEST,
    )
    labels = jnp.where(group_a[:, :, None] == group_b[:, None, :], 1.0, -1.0).astype(jnp.float32)
    return -weight_values * labels * jax.nn.sigmoid(-labels * scores) * scale


def on_device(embeddings, language, sentence_group, pair_mask):
    rows, width = embeddings.shape
    scale = 1.0 / math.sqrt(width)
    lang_count = pair_mask.shape[0]
    weight_table = (pair_mask + pair_mask.T).astype(jnp.float32) * 0.5
    meta = sentence_group * lang_count + language
    device = lax.axis_index(("grp", "dev"))
    own_index = device * rows + jnp.arange(rows, dtype=jnp.int32)

    def piece_terms(piece_rows, piece_meta, start):
        count = piece_rows.shape[0]
        scores = jnp.dot(embeddings, piece_rows.T, preferred_element_type=jnp.float32)[None] * scale
        coef = coefficients(scores, meta[None], piece_meta[None], weight_table, scale)[0]
        column_index = start + jnp.arange(count, dtype=jnp.int32)
        offdiag = (own_index[:, None] != column_index[None, :]).astype(jnp.float32)
        coef = (coef * offdiag).astype(jnp.bfloat16)
        return jnp.dot(coef, piece_rows, preferred_element_type=jnp.float32)

    empty = jnp.zeros((rows, width), jnp.float32)
    total_grad = empty
    piece_rows = lax.all_gather(embeddings, ("grp", "dev"), axis=0, tiled=True)
    piece_meta = lax.all_gather(meta, ("grp", "dev"), axis=0, tiled=True)
    count = piece_rows.shape[0]
    block_rows = 2048
    split_rows = piece_rows.reshape(count // block_rows, block_rows, width)
    split_meta = piece_meta.reshape(count // block_rows, block_rows)

    def scan_block(carry, inputs):
        block_index, block_data, block_meta = inputs
        return (carry + piece_terms(block_data, block_meta, block_index * block_rows), None)

    indices = jnp.arange(count // block_rows, dtype=jnp.int32)
    total_grad, _ = lax.scan(scan_block, total_grad, (indices, split_rows, split_meta))
    return total_grad


def solution(mesh):
    return jax.shard_map(
        on_device,
        mesh=mesh,
        in_specs=(P(("grp", "dev"), None), P(("grp", "dev")), P(("grp", "dev")), P()),
        out_specs=P(("grp", "dev"), None),
        check_vma=False,
    )
```

profile of v0, /device:TPU:0, one launch (start us, length us, event | category | flops | bytes accessed | tf_op | source)
XLA Modules:
  0.0 154.5 jit_solution(4715372799977365501)
XLA Ops:
  6.5 0.7 all-gather.3.cloned.1.call-update
  7.3 0.7 fusion.43
  8.0 71.2 %all-gather = s32[32,1,256]{2,1,0:T(1,128)S(1)} all-gather(s32[1,1,256]{2,1,0:T(1,128)S(1)} %bitcast.72), channel_id=1, replica_groups=mesh['grp'=4,'dev'=8] {'grp','dev'}, dimensions={0}, use_global_device_ids=true | all-gather | bytes 33792 | tf_op jit(solution)/shard_map/all_gather | solution.py:53
  79.3 0.9 copy.6
  80.2 0.8 fusion.42
  81.1 27.6 %all-gather.3.cloned.1.call-done = bf16[8192,768]{1,0:T(8,128)(2,1)} async-done(((bf16[256,768]{1,0:T(8,128)(2,1)}), bf16[8192,768]{1,0:T(8,128)(2,1)}) %all-gather.3.cloned.1.call-update) | async-done | bytes 12582928 | tf_op jit(solution)/shard_map/all_gather | solution.py:52
  108.7 38.0 %while.14 = (s32[]{:T(128)}, f32[256,768]{1,0:T(8,128)S(1)}, s32[4]{0:T(128)S(1)}, s32[256]{0:T(256)S(1)}, f32[109,109]{1,0:T(8,128)S(1)}, /*index=5*/s32[4,2048...) while((s32[]{:T(128)}, f32[256,768]{1,0:T(8,128)S(1)}, ...), condition=%wide.region_1.2_spmd.clone, body=%wide.region_0.1_spmd.clone.sunk | while | flops 2342466816 | bytes 14896207 | solution.py:64
  108.7 0.1 and_select_fusion.6
  108.8 3.1 %fusion.64 = f32[256,2048]{1,0:T(8,128)S(1)} fusion(bf16[256,768]{1,0:T(8,128)(2,1)} %get-tuple-element.328, bf16[4,2048,768]{2,1,0:T(8,128)(2,1)} %get-tuple-element.327, s32[]{:T(128)} %get-tuple-element.307, s32[2048]{0:T(1024)S(1)} %bitcast.70, s32[256]{0:T(256)S(1)} %get-tuple-element.290), kind=kOutput, calls=%fused_computation.20.clone.1 | convolution fusion | flops 809500672 | bytes 5645824 | tf_op jit(solution)/shard_map/while/body/eval_jaxpr/dot_general | solution.py:43
  111.9 0.6 dynamic_slice.60
  113.2 0.3 fusion.65
  113.5 1.6 %fusion.66 = bf16[256,2048]{1,0:T(8,128)(2,1)S(1)} fusion(f32[256,2048]{1,0:T(8,128)S(1)} %fusion.64, f32[256,109]{1,0:T(8,128)S(1)} %fusion.65, s32[2048]{0:T(1024)S(1)} %bitcast.71, s32[2048]{0:T(1024)S(1)} %iota_add_fusion.3, s32[256]{0:T(256)S(1)} %get-tuple-element.290, s32[256]{0:T(256)S(1)} %get-tuple-element.292, s32[2048]{0:T(1024)S(1)} %bitcast.69), kind=kOutput, calls=%fused_computation.19.clone.1 | convolution fusion | flops 690710528 | bytes 3283968 | tf_op jit(solution)/shard_map/while/body/eval_jaxpr/auk,ack->auc/dot_general | solution.py:22
  115.1 3.1 %fusion.67 = f32[256,768]{1,0:T(8,128)S(1)} fusion(bf16[256,2048]{1,0:T(8,128)(2,1)S(1)} %fusion.66, bf16[4,2048,768]{2,1,0:T(8,128)(2,1)} %get-tuple-element.327, s32[]{:T(128)} %get-tuple-element.307, f32[256,768]{1,0:T(8,128)S(1)} %get-tuple-element.308, pred[]{:T(512)S(6)} %compare.3), kind=kOutput, calls=%fused_computation.21.clone.1 | convolution fusion | flops 805699584 | bytes 5767681 | tf_op jit(solution)/shard_map/while/body/eval_jaxpr/dot_general | solution.py:48
  118.2 0.1 and_select_fusion.6
  118.4 3.1 %fusion.64 = f32[256,2048]{1,0:T(8,128)S(1)} fusion(bf16[256,768]{1,0:T(8,128)(2,1)} %get-tuple-element.328, bf16[4,2048,768]{2,1,0:T(8,128)(2,1)} %get-tuple-element.327, s32[]{:T(128)} %get-tuple-element.307, s32[2048]{0:T(1024)S(1)} %bitcast.70, s32[256]{0:T(256)S(1)} %get-tuple-element.290), kind=kOutput, calls=%fused_computation.20.clone.1 | convolution fusion | flops 809500672 | bytes 5645824 | tf_op jit(solution)/shard_map/while/body/eval_jaxpr/dot_general | solution.py:43
  121.5 0.6 dynamic_slice.60
  122.7 0.3 fusion.65
  123.0 1.6 %fusion.66 = bf16[256,2048]{1,0:T(8,128)(2,1)S(1)} fusion(f32[256,2048]{1,0:T(8,128)S(1)} %fusion.64, f32[256,109]{1,0:T(8,128)S(1)} %fusion.65, s32[2048]{0:T(1024)S(1)} %bitcast.71, s32[2048]{0:T(1024)S(1)} %iota_add_fusion.3, s32[256]{0:T(256)S(1)} %get-tuple-element.290, s32[256]{0:T(256)S(1)} %get-tuple-element.292, s32[2048]{0:T(1024)S(1)} %bitcast.69), kind=kOutput, calls=%fused_computation.19.clone.1 | convolution fusion | flops 690710528 | bytes 3283968 | tf_op jit(solution)/shard_map/while/body/eval_jaxpr/auk,ack->auc/dot_general | solution.py:22
  124.6 3.1 %fusion.67 = f32[256,768]{1,0:T(8,128)S(1)} fusion(bf16[256,2048]{1,0:T(8,128)(2,1)S(1)} %fusion.66, bf16[4,2048,768]{2,1,0:T(8,128)(2,1)} %get-tuple-element.327, s32[]{:T(128)} %get-tuple-element.307, f32[256,768]{1,0:T(8,128)S(1)} %get-tuple-element.308, pred[]{:T(512)S(6)} %compare.3), kind=kOutput, calls=%fused_computation.21.clone.1 | convolution fusion | flops 805699584 | bytes 5767681 | tf_op jit(solution)/shard_map/while/body/eval_jaxpr/dot_general | solution.py:48
  127.7 0.1 and_select_fusion.6
  127.9 3.1 %fusion.64 = f32[256,2048]{1,0:T(8,128)S(1)} fusion(bf16[256,768]{1,0:T(8,128)(2,1)} %get-tuple-element.328, bf16[4,2048,768]{2,1,0:T(8,128)(2,1)} %get-tuple-element.327, s32[]{:T(128)} %get-tuple-element.307, s32[2048]{0:T(1024)S(1)} %bitcast.70, s32[256]{0:T(256)S(1)} %get-tuple-element.290), kind=kOutput, calls=%fused_computation.20.clone.1 | convolution fusion | flops 809500672 | bytes 5645824 | tf_op jit(solution)/shard_map/while/body/eval_jaxpr/dot_general | solution.py:43
  131.0 0.6 dynamic_slice.60
  132.2 0.3 fusion.65
  132.5 1.6 %fusion.66 = bf16[256,2048]{1,0:T(8,128)(2,1)S(1)} fusion(f32[256,2048]{1,0:T(8,128)S(1)} %fusion.64, f32[256,109]{1,0:T(8,128)S(1)} %fusion.65, s32[2048]{0:T(1024)S(1)} %bitcast.71, s32[2048]{0:T(1024)S(1)} %iota_add_fusion.3, s32[256]{0:T(256)S(1)} %get-tuple-element.290, s32[256]{0:T(256)S(1)} %get-tuple-element.292, s32[2048]{0:T(1024)S(1)} %bitcast.69), kind=kOutput, calls=%fused_computation.19.clone.1 | convolution fusion | flops 690710528 | bytes 3283968 | tf_op jit(solution)/shard_map/while/body/eval_jaxpr/auk,ack->auc/dot_general | solution.py:22
  134.1 3.1 %fusion.67 = f32[256,768]{1,0:T(8,128)S(1)} fusion(bf16[256,2048]{1,0:T(8,128)(2,1)S(1)} %fusion.66, bf16[4,2048,768]{2,1,0:T(8,128)(2,1)} %get-tuple-element.327, s32[]{:T(128)} %get-tuple-element.307, f32[256,768]{1,0:T(8,128)S(1)} %get-tuple-element.308, pred[]{:T(512)S(6)} %compare.3), kind=kOutput, calls=%fused_computation.21.clone.1 | convolution fusion | flops 805699584 | bytes 5767681 | tf_op jit(solution)/shard_map/while/body/eval_jaxpr/dot_general | solution.py:48
  137.2 0.1 and_select_fusion.6
  137.4 3.1 %fusion.64 = f32[256,2048]{1,0:T(8,128)S(1)} fusion(bf16[256,768]{1,0:T(8,128)(2,1)} %get-tuple-element.328, bf16[4,2048,768]{2,1,0:T(8,128)(2,1)} %get-tuple-element.327, s32[]{:T(128)} %get-tuple-element.307, s32[2048]{0:T(1024)S(1)} %bitcast.70, s32[256]{0:T(256)S(1)} %get-tuple-element.290), kind=kOutput, calls=%fused_computation.20.clone.1 | convolution fusion | flops 809500672 | bytes 5645824 | tf_op jit(solution)/shard_map/while/body/eval_jaxpr/dot_general | solution.py:43
  140.5 0.6 dynamic_slice.60
  141.7 0.3 fusion.65
  142.0 1.6 %fusion.66 = bf16[256,2048]{1,0:T(8,128)(2,1)S(1)} fusion(f32[256,2048]{1,0:T(8,128)S(1)} %fusion.64, f32[256,109]{1,0:T(8,128)S(1)} %fusion.65, s32[2048]{0:T(1024)S(1)} %bitcast.71, s32[2048]{0:T(1024)S(1)} %iota_add_fusion.3, s32[256]{0:T(256)S(1)} %get-tuple-element.290, s32[256]{0:T(256)S(1)} %get-tuple-element.292, s32[2048]{0:T(1024)S(1)} %bitcast.69), kind=kOutput, calls=%fused_computation.19.clone.1 | convolution fusion | flops 690710528 | bytes 3283968 | tf_op jit(solution)/shard_map/while/body/eval_jaxpr/auk,ack->auc/dot_general | solution.py:22
  143.6 3.1 %fusion.67 = f32[256,768]{1,0:T(8,128)S(1)} fusion(bf16[256,2048]{1,0:T(8,128)(2,1)S(1)} %fusion.66, bf16[4,2048,768]{2,1,0:T(8,128)(2,1)} %get-tuple-element.327, s32[]{:T(128)} %get-tuple-element.307, f32[256,768]{1,0:T(8,128)S(1)} %get-tuple-element.308, pred[]{:T(512)S(6)} %compare.3), kind=kOutput, calls=%fused_computation.21.clone.1 | convolution fusion | flops 805699584 | bytes 5767681 | tf_op jit(solution)/shard_map/while/body/eval_jaxpr/dot_general | solution.py:48
  146.7 0.9 copy-done
  (18 shorter events, 0.3 us)
Async XLA Ops:
  6.5 102.2 %all-gather.3.cloned.1.call-start = ((), (), s32[]{:S(2)}) async-start(), calls=%async_computation | async-start | bytes 12976128 | tf_op jit(solution)/shard_map/all_gather | solution.py:52
  146.7 0.9 copy-start
Sparse Core Ops, SparseCore 0:
  10.3 98.3 all-gather.2
where the time goes:
time: 155 us; the launch traced here: 154 us
  blocking collectives  71.2 us (46%)
  matrix products  32.2 us (21%)
  waiting for transfers between devices  28.4 us (18%)
  between operations  13.4 us (9%)
  local copies, waits for them, and re-layouts  4.3 us (3%)
  loops' own time  2.78 us (2%)
  other arithmetic  2.13 us (1%)
    all_gather x1, blocking collectives, on_device(): piece_meta = lax.all_gather(meta, ('grp', 'dev'), axis=0, tiled=True)  71.2 us
    all_gather x1, waiting for transfers between devices, on_device(): piece_rows = lax.all_gather(embeddings, ('grp', 'dev'), axis=0, tiled=True)  27.6 us
    dot_general x4, matrix products, piece_terms(): jnp.dot(embeddings, piece_rows.T, preferred_element_type=jnp.float32)[None]  12.4 us
    dot_general x4, matrix products, piece_terms(): return jnp.dot(coef, piece_rows, preferred_element_type=jnp.float32)  12.3 us
    dot_general x4, matrix products, coefficients(): jnp.einsum('auk,ack->auc', weight_applied_terms, second_language_indicato...  6.48 us
  transfers between devices with their start and end apart: 1, of which 1 were waited for; matrix products, arithmetic and copies ran while one was open for 2% of the time, Pallas kernels for 0%

commit v1 on v0

v1 whole, which is shorter than its diff:
```python
import functools
import math

import jax
import jax.numpy as jnp
from jax import lax
from jax.experimental import pallas as pl
from jax.experimental.pallas import tpu as pltpu
from jax.sharding import PartitionSpec as P

MESH = pl.DeviceIdType.MESH


def kernel(groups, devs, e_hbm, m_hbm, mask_ref, out_ref, buf, mbuf, wr, gcol, send_sem, recv_sem, own_sem):
    rows, width = buf.shape[1], buf.shape[2]
    langs = mask_ref.shape[0]
    depth = devs // 2
    scale = 1.0 / math.sqrt(width)
    g, d = lax.axis_index("grp"), lax.axis_index("dev")
    core, y = g % 2, g // 2
    x, z = d % 2, d // 2
    me = g * devs + d
    half = rows // 2

    def block(yy, cc, zz, xx):
        return (yy * 2 + cc) * devs + zz * 2 + xx

    def view(ch, b):
        if ch == 0:
            return buf.at[b, pl.ds(0, half)]
        if ch == 1:
            return buf.at[b, pl.ds(half, half)]
        return mbuf.at[b]

    x_second = (True, False, True)
    channels = range(3)

    own_copies = [
        pltpu.make_async_copy(e_hbm, buf.at[me], own_sem.at[0]),
        pltpu.make_async_copy(m_hbm, mbuf.at[me], own_sem.at[1]),
    ]
    for c in own_copies:
        c.start()

    to_x, to_y, to_core = (g, d + 1 - 2 * x), (g + 2 - 4 * y, d), (g + 1 - 2 * core, d)
    up, down = (g, d + 2), (g, d - 2)
    has_up, has_down = z + 1 < depth, z > 0
    barrier = pltpu.get_barrier_semaphore()
    for target in (to_x, to_y, to_core):
        pl.semaphore_signal(barrier, inc=1, device_id=target, device_id_type=MESH)

    @pl.when(has_up)
    def _():
        pl.semaphore_signal(barrier, inc=1, device_id=up, device_id_type=MESH)

    @pl.when(has_down)
    def _():
        pl.semaphore_signal(barrier, inc=1, device_id=down, device_id_type=MESH)

    pl.semaphore_wait(barrier, 3 + has_up.astype(jnp.int32) + has_down.astype(jnp.int32))

    def copy(ch, way, b, target):
        return pltpu.make_async_remote_copy(
            src_ref=view(ch, b),
            dst_ref=view(ch, b),
            send_sem=send_sem.at[ch, way, b],
            recv_sem=recv_sem.at[ch, b],
            device_id=target,
            device_id_type=MESH,
        )

    def arrived(ch, b):
        copy(ch, 0, b, to_core).wait_recv()

    def act(ch, way, b, target, start):
        c = copy(ch, way, b, target)
        if start:
            c.start()
        else:
            c.wait_send()

    short = jnp.minimum(z, depth - 1 - z)
    long_sign = jnp.where(z * 2 < depth, 1, -1)

    def line(k):
        near = (k + 1) // 2
        sign = jnp.where(k % 2 == 1, long_sign, -long_sign)
        return jnp.where(k <= 2 * short, z + sign * near, z + long_sign * (k - short))

    def first(k, start):
        zz = line(k)
        b = block(y, core, zz, x)
        for ch in channels:
            if start:

                @pl.when(k > 0)
                def _():
                    arrived(ch, b)

            @pl.when(jnp.logical_and(zz <= z, has_up))
            def _():
                act(ch, 0, b, up, start)

            @pl.when(jnp.logical_and(zz >= z, has_down))
            def _():
                act(ch, 1, b, down, start)

            act(ch, 2, b, to_x if x_second[ch] else to_y, start)
            act(ch, 3, b, to_y if x_second[ch] else to_x, start)
            act(ch, 4, b, to_core, start)

    def second(k, start):
        zz = line(k)
        for ch in channels:
            b = block(y, core, zz, 1 - x) if x_second[ch] else block(1 - y, core, zz, x)
            if start:
                arrived(ch, b)
            act(ch, 3, b, to_y if x_second[ch] else to_x, start)
            act(ch, 4, b, to_core, start)

    def third(k, start):
        zz = line(k)
        for last in range(2):
            for ch in channels:
                if last:
                    b = block(1 - y, core, zz, 1 - x)
                else:
                    b = block(1 - y, core, zz, x) if x_second[ch] else block(y, core, zz, 1 - x)
                if start:
                    arrived(ch, b)
                act(ch, 4, b, to_core, start)

    for c in own_copies:
        c.wait()
    first(0, True)

    lang_axis = lax.broadcasted_iota(jnp.int32, (langs, rows), 0)
    table = mask_ref[...].astype(jnp.float32)
    table = ((table + table.T) * 0.5).astype(jnp.bfloat16)
    own_hot = (lang_axis == mbuf[me, 0:1, :]).astype(jnp.float32).astype(jnp.bfloat16)
    wr[...] = lax.dot_general(
        own_hot, table, (((0,), (0,)), ((), ())), preferred_element_type=jnp.float32
    ).astype(jnp.bfloat16)
    gcol[...] = jnp.broadcast_to(mbuf[me, 1:2, :].astype(jnp.float32), (128, rows)).T
    out_ref[...] = jnp.zeros_like(out_ref)

    def compute(b):
        cols = buf[b]
        scores = lax.dot_general(
            buf[me], cols, (((1,), (1,)), ((), ())), preferred_element_type=jnp.float32
        )
        hot = (lang_axis == mbuf[b, 0:1, :]).astype(jnp.float32).astype(jnp.bfloat16)
        weight = jnp.dot(wr[...], hot, preferred_element_type=jnp.float32)
        own_group = jnp.concatenate([gcol[...]] * (rows // 128), axis=1)
        same = own_group == mbuf[b, 1:2, :].astype(jnp.float32)
        power = jnp.minimum(jnp.where(same, scores, -scores) * (scale * math.log2(math.e)), 127.9)
        signed = jnp.where(same, -weight, weight)
        coef = signed * (scale / (1.0 + jnp.exp2(power)))
        apart = lax.broadcasted_iota(jnp.int32, (rows, rows), 0) - lax.broadcasted_iota(
            jnp.int32, (rows, rows), 1
        )
        coef = jnp.where(apart == (b - me) * rows, 0.0, coef).astype(jnp.bfloat16)
        out_ref[...] += jnp.dot(coef, cols, preferred_element_type=jnp.float32)

    def step(k, carry):
        @pl.when(k < depth)
        def _():
            first(k, True)

        @pl.when(k <= depth)
        def _():
            second(k - 1, True)

        @pl.when(k >= 2)
        def _():
            third(k - 2, True)
            zz = line(k - 2)

            def one(j, carry):
                yy = (y + j // 2) % 2
                xx = (x + j) % 2
                cc = (core + j // 4) % 2
                b = block(yy, cc, zz, xx)

                @pl.when(j >= 4)
                def _():
                    for ch in channels:
                        arrived(ch, b)

                compute(b)
                return carry

            lax.fori_loop(0, 8, one, 0)

        return carry

    lax.fori_loop(1, depth + 2, step, 0)

    def drain(k, carry):
        first(k, False)
        second(k, False)
        third(k, False)
        return carry

    lax.fori_loop(0, depth, drain, 0)


def on_device(groups, devs, embeddings, language, sentence_group, pair_mask):
    rows, width = embeddings.shape
    count = groups * devs
    langs = pair_mask.shape[0]
    meta = jnp.stack([language, sentence_group])
    return pl.pallas_call(
        functools.partial(kernel, groups, devs),
        out_shape=jax.ShapeDtypeStruct((rows, width), jnp.float32),
        in_specs=[
            pl.BlockSpec(memory_space=pl.ANY),
            pl.BlockSpec(memory_space=pl.ANY),
            pl.BlockSpec(memory_space=pltpu.VMEM),
        ],
        out_specs=pl.BlockSpec(memory_space=pltpu.VMEM),
        scratch_shapes=[
            pltpu.VMEM((count, rows, width), jnp.bfloat16),
            pltpu.VMEM((count, 2, rows), jnp.int32),
            pltpu.VMEM((rows, langs), jnp.bfloat16),
            pltpu.VMEM((rows, 128), jnp.float32),
            pltpu.SemaphoreType.DMA((3, 5, count)),
            pltpu.SemaphoreType.DMA((3, count)),
            pltpu.SemaphoreType.DMA((2,)),
        ],
        compiler_params=pltpu.CompilerParams(
            collective_id=0, has_side_effects=True, vmem_limit_bytes=64 * 1000 * 1000
        ),
    )(embeddings, meta, pair_mask)


def solution(mesh):
    groups, devs = mesh.shape["grp"], mesh.shape["dev"]
    return jax.shard_map(
        functools.partial(on_device, groups, devs),
        mesh=mesh,
        in_specs=(P(("grp", "dev"), None), P(("grp", "dev")), P(("grp", "dev")), P()),
        out_specs=P(("grp", "dev"), None),
        check_vma=False,
    )
```

time: 155 us -> 77.4 us (0.50)
  Pallas kernels: 0 us -> 73.8 us
  blocking collectives: 71.2 us -> 0 us
  matrix products: 32.2 us -> 0 us
  waiting for transfers between devices: 28.4 us -> 0 us
  between operations: 13.4 us -> 0.01 us
  loops' own time: 2.78 us -> 0 us
    pallas_call x0 -> x1, Pallas kernels: none -> 73.8 us  [on_device(): pl.pallas_call(functools.partial(kernel, groups, devs), out_shape=jax.Sha...]
    all_gather x1 -> x0, blocking collectives: 71.2 us -> none  [on_device(): piece_meta = lax.all_gather(meta, ('grp', 'dev'), axis=0, tiled=True)]
    dot_general x16 -> x0, matrix products: 32.2 us -> none  [the longest x4 12.4 us: piece_terms(): jnp.dot(embeddings, piece_rows.T, preferred_element_type=jnp.float32)[None]]
    all_gather x1 -> x0, waiting for transfers between devices: 27.6 us -> none  [on_device(): piece_rows = lax.all_gather(embeddings, ('grp', 'dev'), axis=0, tiled=True)]
    another operation x1 -> x0, loops' own time: 2.78 us -> none  [on_device(): lax.scan(scan_block, total_grad, (indices, split_rows, split_meta))]
    dynamic_slice x4 -> x0, local copies, waits for them, and re-layouts: 2.49 us -> none  [on_device(): lax.scan(scan_block, total_grad, (indices, split_rows, split_meta))]
  transfers between devices with their start and end apart: 1 -> 0, of which waited for: 1 -> 0; matrix products, arithmetic and copies ran while one was open for 2% -> 0% of each run, Pallas kernels for 0% -> 0%
where the time goes in v1:
time: 77.4 us; the launch traced here: 77.2 us
  Pallas kernels  73.8 us (95%)
  local copies, waits for them, and re-layouts  2.76 us (4%)
    pallas_call x1, Pallas kernels, on_device(): pl.pallas_call(functools.partial(kernel, groups, devs), out_shape=jax.Sha...  73.8 us
    unnamed x5, local copies, waits for them, and re-layouts  2.76 us

profile of v1, /device:TPU:0, one launch (start us, length us, event | category | flops | bytes accessed | tf_op | source)
XLA Modules:
  0.0 77.2 jit_solution(16111069526233434096)
XLA Ops:
  0.0 0.0 copy-start.1
  0.0 0.0 copy-start
  0.0 0.7 copy-done.1
  0.7 0.0 copy-done
  0.7 0.6 pad_add_fusion.m_hbm
  1.3 73.8 %shard_map.46 = f32[256,768]{1,0:T(8,128)} custom-call(bf16[256,768]{1,0:T(8,128)(2,1)} %e_hbm.1, s32[2,256]{1,0:T(2,128)} %pad_add_fusion.m_hbm, s32[109,109]{1,0:T(8,128)} %mask_ref.1), custom_call_target="tpu_custom_call" | custom-call | tf_op jit(solution)/shard_map/pallas_call | solution.py:213
  75.1 2.1 %copy.6 = f32[256,768]{1,0:T(8,128)} copy(f32[256,768]{1,0:T(8,128)} %shard_map.46) | data formatting | bytes 1572864
Async XLA Ops:
  0.0 0.7 copy-start.1
  0.0 0.7 copy-start

commit v2 on v1

--- a/solution.py
+++ b/solution.py
@@ -118,17 +118,16 @@
             act(ch, 3, b, to_y if x_second[ch] else to_x, start)
             act(ch, 4, b, to_core, start)
 
-    def third(k, start):
-        zz = line(k)
-        for last in range(2):
-            for ch in channels:
-                if last:
-                    b = block(1 - y, core, zz, 1 - x)
-                else:
-                    b = block(1 - y, core, zz, x) if x_second[ch] else block(y, core, zz, 1 - x)
-                if start:
-                    arrived(ch, b)
-                act(ch, 4, b, to_core, start)
+    def third(k, last, start):
+        zz = line(k)
+        for ch in channels:
+            if last:
+                b = block(1 - y, core, zz, 1 - x)
+            else:
+                b = block(1 - y, core, zz, x) if x_second[ch] else block(y, core, zz, 1 - x)
+            if start:
+                arrived(ch, b)
+            act(ch, 4, b, to_core, start)
 
     for c in own_copies:
         c.wait()
@@ -144,23 +143,64 @@
     gcol[...] = jnp.broadcast_to(mbuf[me, 1:2, :].astype(jnp.float32), (128, rows)).T
     out_ref[...] = jnp.zeros_like(out_ref)
 
-    def compute(b):
-        cols = buf[b]
+    own_group = jnp.concatenate([gcol[...]] * (rows // 128), axis=1)
+
+    def coefficients(b, diagonal):
         scores = lax.dot_general(
-            buf[me], cols, (((1,), (1,)), ((), ())), preferred_element_type=jnp.float32
+            buf[me], buf[b], (((1,), (1,)), ((), ())), preferred_element_type=jnp.float32
         )
         hot = (lang_axis == mbuf[b, 0:1, :]).astype(jnp.float32).astype(jnp.bfloat16)
         weight = jnp.dot(wr[...], hot, preferred_element_type=jnp.float32)
-        own_group = jnp.concatenate([gcol[...]] * (rows // 128), axis=1)
         same = own_group == mbuf[b, 1:2, :].astype(jnp.float32)
         power = jnp.minimum(jnp.where(same, scores, -scores) * (scale * math.log2(math.e)), 127.9)
         signed = jnp.where(same, -weight, weight)
         coef = signed * (scale / (1.0 + jnp.exp2(power)))
-        apart = lax.broadcasted_iota(jnp.int32, (rows, rows), 0) - lax.broadcasted_iota(
-            jnp.int32, (rows, rows), 1
-        )
-        coef = jnp.where(apart == (b - me) * rows, 0.0, coef).astype(jnp.bfloat16)
-        out_ref[...] += jnp.dot(coef, cols, preferred_element_type=jnp.float32)
+        if diagonal:
+            apart = lax.broadcasted_iota(jnp.int32, (rows, rows), 0) - lax.broadcasted_iota(
+                jnp.int32, (rows, rows), 1
+            )
+            coef = jnp.where(apart == (b - me) * rows, 0.0, coef)
+        return coef.astype(jnp.bfloat16)
+
+    def compute(blocks, diagonal=False):
+        total = None
+        for b in blocks:
+            part = jnp.dot(
+                coefficients(b, diagonal), buf[b], preferred_element_type=jnp.float32
+            )
+            total = part if total is None else total + part
+        out_ref[...] += total
+
+    def near_pair(k):
+        zz = line(k)
+        own, other = block(y, core, zz, x), block(y, 1 - core, zz, x)
+        for ch in channels:
+            arrived(ch, other)
+        compute((own, other), True)
+
+    def side_pair(k, cc, wait):
+        zz = line(k)
+        pair = (block(y, cc, zz, 1 - x), block(1 - y, cc, zz, x))
+
+        if wait is not None:
+
+            @pl.when(wait)
+            def _():
+                for b in pair:
+                    for ch in channels:
+                        arrived(ch, b)
+
+        compute(pair)
+
+    def far_block(k, cc, wait):
+        b = block(1 - y, cc, line(k), 1 - x)
+
+        @pl.when(wait)
+        def _():
+            for ch in channels:
+                arrived(ch, b)
+
+        compute((b,))
 
     def step(k, carry):
         @pl.when(k < depth)
@@ -170,27 +210,24 @@
         @pl.when(k <= depth)
         def _():
             second(k - 1, True)
+            near_pair(k - 1)
 
         @pl.when(k >= 2)
         def _():
-            third(k - 2, True)
-            zz = line(k - 2)
-
-            def one(j, carry):
-                yy = (y + j // 2) % 2
-                xx = (x + j) % 2
-                cc = (core + j // 4) % 2
-                b = block(yy, cc, zz, xx)
-
-                @pl.when(j >= 4)
-                def _():
-                    for ch in channels:
-                        arrived(ch, b)
-
-                compute(b)
+            third(k - 2, 0, True)
+
+            def side(j, carry):
+                side_pair(k - 2, (core + j) % 2, j > 0)
                 return carry
 
-            lax.fori_loop(0, 8, one, 0)
+            lax.fori_loop(0, 2, side, 0)
+            third(k - 2, 1, True)
+
+            def far(j, carry):
+                far_block(k - 2, (core + j) % 2, j > 0)
+                return carry
+
+            lax.fori_loop(0, 2, far, 0)
 
         return carry
 
@@ -199,7 +236,8 @@
     def drain(k, carry):
         first(k, False)
         second(k, False)
-        third(k, False)
+        third(k, 0, False)
+        third(k, 1, False)
         return carry
 
     lax.fori_loop(0, depth, drain, 0)

time: 77.4 us -> 69.1 us (0.89)
  Pallas kernels: 73.8 us -> 65.2 us
    pallas_call x1, Pallas kernels: 73.8 us -> 65.2 us  [on_device(): pl.pallas_call(functools.partial(kernel, groups, devs), out_shape=jax.Sha...]
where the time goes in v2:
time: 69.1 us; the launch traced here: 68.6 us
  Pallas kernels  65.2 us (94%)
  local copies, waits for them, and re-layouts  2.76 us (4%)
    pallas_call x1, Pallas kernels, on_device(): pl.pallas_call(functools.partial(kernel, groups, devs), out_shape=jax.Sha...  65.2 us
    unnamed x5, local copies, waits for them, and re-layouts  2.76 us

profile of v2, /device:TPU:0, one launch (start us, length us, event | category | flops | bytes accessed | tf_op | source)
XLA Modules:
  0.0 68.6 jit_solution(16880292982457828690)
XLA Ops:
  0.0 0.0 copy-start.1
  0.0 0.0 copy-start
  0.0 0.7 copy-done.1
  0.7 0.0 copy-done
  0.7 0.6 pad_add_fusion.m_hbm
  1.3 65.2 %shard_map.46 = f32[256,768]{1,0:T(8,128)} custom-call(bf16[256,768]{1,0:T(8,128)(2,1)} %e_hbm.1, s32[2,256]{1,0:T(2,128)} %pad_add_fusion.m_hbm, s32[109,109]{1,0:T(8,128)} %mask_ref.1), custom_call_target="tpu_custom_call" | custom-call | tf_op jit(solution)/shard_map/pallas_call | solution.py:251
  66.5 2.1 %copy.6 = f32[256,768]{1,0:T(8,128)} copy(f32[256,768]{1,0:T(8,128)} %shard_map.46) | data formatting | bytes 1572864
Async XLA Ops:
  0.0 0.7 copy-start.1
  0.0 0.7 %copy-start = (s32[256]{0:T(256)S(1)}, s32[256]{0:T(256)}, u32[]{:S(2)}) copy-start(s32[256]{0:T(256)} %param.6) | copy-start | bytes 3076

commit v3 on v2

--- a/solution.py
+++ b/solution.py
@@ -11,7 +11,7 @@
 MESH = pl.DeviceIdType.MESH
 
 
-def kernel(groups, devs, e_hbm, m_hbm, mask_ref, out_ref, buf, mbuf, wr, gcol, send_sem, recv_sem, own_sem):
+def kernel(groups, devs, e_hbm, l_hbm, g_hbm, mask_ref, out_ref, buf, mbuf, wr, gcol, send_sem, recv_sem, own_sem):
     rows, width = buf.shape[1], buf.shape[2]
     langs = mask_ref.shape[0]
     depth = devs // 2
@@ -37,7 +37,8 @@
 
     own_copies = [
         pltpu.make_async_copy(e_hbm, buf.at[me], own_sem.at[0]),
-        pltpu.make_async_copy(m_hbm, mbuf.at[me], own_sem.at[1]),
+        pltpu.make_async_copy(l_hbm, mbuf.at[me, pl.ds(0, 1)], own_sem.at[1]),
+        pltpu.make_async_copy(g_hbm, mbuf.at[me, pl.ds(1, 1)], own_sem.at[2]),
     ]
     for c in own_copies:
         c.start()
@@ -247,11 +248,11 @@
     rows, width = embeddings.shape
     count = groups * devs
     langs = pair_mask.shape[0]
-    meta = jnp.stack([language, sentence_group])
     return pl.pallas_call(
         functools.partial(kernel, groups, devs),
         out_shape=jax.ShapeDtypeStruct((rows, width), jnp.float32),
         in_specs=[
+            pl.BlockSpec(memory_space=pl.ANY),
             pl.BlockSpec(memory_space=pl.ANY),
             pl.BlockSpec(memory_space=pl.ANY),
             pl.BlockSpec(memory_space=pltpu.VMEM),
@@ -264,12 +265,12 @@
             pltpu.VMEM((rows, 128), jnp.float32),
             pltpu.SemaphoreType.DMA((3, 5, count)),
             pltpu.SemaphoreType.DMA((3, count)),
-            pltpu.SemaphoreType.DMA((2,)),
+            pltpu.SemaphoreType.DMA((3,)),
         ],
         compiler_params=pltpu.CompilerParams(
             collective_id=0, has_side_effects=True, vmem_limit_bytes=64 * 1000 * 1000
         ),
-    )(embeddings, meta, pair_mask)
+    )(embeddings, language.reshape(1, rows), sentence_group.reshape(1, rows), pair_mask)
 
 
 def solution(mesh):

time: 69.1 us -> 67.8 us (0.981)
  local copies, waits for them, and re-layouts: 2.76 us -> 2.06 us
    unnamed x5 -> x1, local copies, waits for them, and re-layouts: 2.76 us -> 2.06 us
where the time goes in v3:
time: 67.8 us; the launch traced here: 67.3 us
  Pallas kernels  65.2 us (96%)
  local copies, waits for them, and re-layouts  2.06 us (3%)
    pallas_call x1, Pallas kernels, on_device(): pl.pallas_call(functools.partial(kernel, groups, devs), out_shape=jax.Sha...  65.2 us
    unnamed x1, local copies, waits for them, and re-layouts  2.06 us

profile of v3, /device:TPU:0, one launch (start us, length us, event | category | flops | bytes accessed | tf_op | source)
XLA Modules:
  0.0 67.3 jit_solution(4507212051950934875)
XLA Ops:
  0.0 65.2 %shard_map.46 = f32[256,768]{1,0:T(8,128)} custom-call(bf16[256,768]{1,0:T(8,128)(2,1)} %e_hbm.1, s32[1,256]{1,0:T(1,128)} %bitcast.2, s32[1,256]{1,0:T(1,128)} %bitcast.3, s32[109,109]{1,0:T(8,128)} %mask_ref.1), custom_call_target="tpu_custom_call" | custom-call | tf_op jit(solution)/shard_map/pallas_call | solution.py:251
  65.2 2.1 %copy.6 = f32[256,768]{1,0:T(8,128)} copy(f32[256,768]{1,0:T(8,128)} %shard_map.46) | data formatting | bytes 1572864
